TPU v7x, 32 devices: a whole 2x2x4 slice. The times are simulated.
32 devices in a mesh: ia: 2 (over y), ja: 4 (over z), ka: 4 (over x, core).
Axes of the slice: x: 2, y: 2, z: 4, core: 2. Of those that a mesh axis runs over, the one named last changes fastest.
Arguments:
- blocks: bfloat16 [256, 64, 4096], P(('ia', 'ja', 'ka')), may hold values from -12 to 12
- coords: int32 [256, 3], P(('ia', 'ja', 'ka')), may hold values from 0 to 63, as said below
- factor_one: float32 [2048, 512], P('ia'), may hold values from -1.2 to 1.2
- factor_two: float32 [4096, 512], P('ja'), may hold values from -1.2 to 1.2
- factor_three: float32 [4096, 512], P('ka'), may hold values from -1.2 to 1.2
Outputs:
- swept_one: float32 [2048, 512], P('ia')
- swept_two: float32 [4096, 512], P('ja')
- swept_three: float32 [4096, 512], P('ka')
Inputs may be any that keep to these rules, and one draw needn't show every extreme that they name: Row n of coords holds the three block coordinates of block n. The 8 rows of one device of ia+ja+ka (aligned blocks of 8 rows, devices in the order ia, ja, ka) have their second coordinate within that device's ja range (16 * ja to 16 * ja + 15) and their third within its ka range; at most 8 of them have a first coordinate within any one index of ia's range of 16; in every group of devices that share ja and ka, some index of ia receives exactly 8 from each device of the group. The same block may be listed more than once.
All inputs are finite; a program needn't handle non-finite values.
Results may differ from a plain program's by a relative error of at most 0.0028.
Values may be sent and summed in bfloat16 or wider, within the bound.
A program may use at most 64 MiB of HBM per device.

v0:
```python
import jax
import jax.numpy as jnp
from jax import lax
from jax.sharding import PartitionSpec as P

STEP_SIZE = 0.01
einsum_forms = (
    ("qk,rk->qrk", "pk,qrk->pqr", "pqr,qrk->pk"),
    ("pk,rk->prk", "qk,prk->pqr", "pqr,prk->qk"),
    ("pk,qk->pqk", "rk,pqk->pqr", "pqr,pqk->rk"),
)
other_modes = ((1, 2), (0, 2), (0, 1))


def block_gradient(cube, rows, mode):
    first, second = other_modes[mode]
    outer_form, model_form, grad_form = einsum_forms[mode]
    khatri = jnp.einsum(
        outer_form, rows[first].astype(jnp.float32), rows[second].astype(jnp.float32)
    ).astype(jnp.bfloat16)
    model = jnp.einsum(model_form, rows[mode], khatri, preferred_element_type=jnp.float32)
    misfit = (cube.astype(jnp.float32) - model).astype(jnp.bfloat16)
    return jnp.einsum(grad_form, misfit, khatri, preferred_element_type=jnp.float32)


def accumulate(blocks, coords, factors, starts, live, mode, height):
    edge = blocks.shape[1]
    width = factors[0].shape[1]

    def visit(index, total):

        def add(running):
            place = coords[index]
            rows = tuple(
                (
                    lax.dynamic_slice_in_dim(factors[f], place[f] * edge - starts[f], edge, 0)
                    for f in range(3)
                )
            )
            cube = blocks[index].reshape(edge, edge, edge)
            term = block_gradient(cube, rows, mode)
            offset = place[mode] * edge - starts[mode]
            current = lax.dynamic_slice_in_dim(running, offset, edge, 0)
            return lax.dynamic_update_slice_in_dim(running, current + term, offset, 0)

        return lax.cond(live[index], add, lambda running: running, total)

    empty = jnp.zeros((height, width), jnp.float32)
    return lax.fori_loop(0, blocks.shape[0], visit, empty)


def block_slots(coords, count, per_pair, held_rows):
    target = coords[:, 0] // held_rows
    same = target[:, None] == target[None, :]
    earlier = jnp.arange(count)[None, :] < jnp.arange(count)[:, None]
    before = jnp.sum((same & earlier).astype(jnp.int32), axis=1)
    return target * per_pair + before


def serve_rows(incoming, factor, edge, held_rows):
    width = factor.shape[1]
    within = incoming - lax.axis_index("ia") * held_rows
    safe_rows = jnp.clip(within, 0, held_rows - 1)
    picked = factor.astype(jnp.bfloat16).reshape(held_rows, edge, width)[safe_rows]
    return lax.all_to_all(picked, "ia", split_axis=0, concat_axis=0, tiled=True)


def per_device(blocks, coords, factor_one, factor_two, factor_three):
    edge = blocks.shape[1]
    count = blocks.shape[0]
    groups = lax.axis_size("ia")
    span_one = factor_one.shape[0]
    span_two = factor_two.shape[0]
    span_three = factor_three.shape[0]
    width = factor_one.shape[1]
    held_rows = span_one // edge
    per_pair = max(2, 2 * count // groups)
    start_two = lax.axis_index("ja") * span_two
    start_three = lax.axis_index("ka") * span_three
    slot = block_slots(coords, count, per_pair, held_rows)
    all_slots = groups * per_pair
    wanted = jnp.full((all_slots,), -1, jnp.int32).at[slot].set(coords[:, 0])
    incoming = lax.all_to_all(wanted, "ia", split_axis=0, concat_axis=0, tiled=True)
    fetched = serve_rows(incoming, factor_one, edge, held_rows).reshape(all_slots * edge, width)
    places = coords.at[:, 0].set(slot)
    live = jnp.ones((count,), jnp.bool_)
    slot_terms = accumulate(
        blocks,
        places,
        (fetched, factor_two.astype(jnp.bfloat16), factor_three.astype(jnp.bfloat16)),
        (0, start_two, start_three),
        live,
        0,
        all_slots * edge,
    )
    returned = lax.all_to_all(
        slot_terms.reshape(all_slots, edge, width), "ia", split_axis=0, concat_axis=0, tiled=True
    )
    within = incoming - lax.axis_index("ia") * held_rows
    selector = (within[None, :] == jnp.arange(held_rows)[:, None]).astype(jnp.float32)
    first_part = jnp.dot(
        selector,
        returned.reshape(all_slots, edge * width),
        precision=lax.Precision.HIGHEST,
        preferred_element_type=jnp.float32,
    ).reshape(span_one, width)
    first_part = lax.psum(first_part, ("ja", "ka"))
    factor_one = factor_one + STEP_SIZE * first_part
    first_rows = serve_rows(incoming, factor_one, edge, held_rows).reshape(
        groups * per_pair * edge, width
    )
    first_start = 0
    second_part = accumulate(
        blocks,
        places,
        (first_rows, factor_two.astype(jnp.bfloat16), factor_three.astype(jnp.bfloat16)),
        (first_start, start_two, start_three),
        live,
        1,
        span_two,
    )
    second_part = lax.psum(second_part, ("ia", "ka"))
    factor_two = factor_two + STEP_SIZE * second_part
    third_part = accumulate(
        blocks,
        places,
        (first_rows, factor_two.astype(jnp.bfloat16), factor_three.astype(jnp.bfloat16)),
        (first_start, start_two, start_three),
        live,
        2,
        span_three,
    )
    third_part = lax.psum(third_part, ("ia", "ja"))
    factor_three = factor_three + STEP_SIZE * third_part
    return (factor_one, factor_two, factor_three)


def solution(mesh):
    in_specs = (
        P(("ia", "ja", "ka"), None, None),
        P(("ia", "ja", "ka"), None),
        P("ia", None),
        P("ja", None),
        P("ka", None),
    )
    out_specs = (P("ia", None), P("ja", None), P("ka", None))
    return jax.shard_map(
        per_device, mesh=mesh, in_specs=in_specs, out_specs=out_specs, check_vma=False
    )
```

profile of v0, /device:TPU:0, one launch (start us, length us, event | category | flops | bytes accessed | tf_op | source)
XLA Modules:
  0.0 621.7 jit_solution(2798835930513432250)
XLA Ops:
  27.9 8.9 %all-to-all-done.1 = bf16[16,64,512]{2,1,0:T(8,128)(2,1)S(1)} async-done(((bf16[16,64,512]{2,1,0:T(8,128)(2,1)}), bf16[16,64,512]{2,1,0:T(8,128)(2,1)S(1)}, u32[]{:S(2)}, u32[]{:S(2)}) %all-to-all-start.1) | async-done | bytes 1048608 | tf_op jit(solution)/shard_map/all_to_all | solution.py:65
  38.3 86.3 %while.40 = (s32[]{:T(128)}, f32[1024,512]{1,0:T(8,128)}, s32[8,3]{0,1:T(4,128)S(1)}, bf16[8,64,4096]{2,1,0:T(8,128)(2,1)}, bf16[1024,512]{1,0:T(8,128)(2,1)S(1)...) while((s32[]{:T(128)}, f32[1024,512]{1,0:T(8,128)}, ...), condition=%wide.region_4.5_spmd, body=%wide.region_3.4_spmd.sunk | while | flops 546144256 | bytes 15402399 | solution.py:49
  44.1 5.0 fusion.118
  54.8 5.0 fusion.118
  65.6 5.0 fusion.118
  76.4 5.0 fusion.118
  87.2 5.0 fusion.118
  98.0 5.0 fusion.118
  108.8 5.0 fusion.118
  119.6 5.0 fusion.118
  128.5 23.1 %all-to-all-done.2 = f32[16,64,512]{2,1,0:T(8,128)S(1)} async-done(((f32[16,64,512]{2,1,0:T(8,128)}), f32[16,64,512]{2,1,0:T(8,128)S(1)}, u32[]{:S(2)}, u32[]{:S(2)}) %all-to-all-start.2) | async-done | bytes 2097184 | tf_op jit(solution)/shard_map/all_to_all | solution.py:96
  155.5 98.7 %all-reduce.4.cloned.1.call-done = f32[1024,512]{1,0:T(8,128)} async-done(((f32[1024,512]{1,0:T(8,128)}), f32[1024,512]{1,0:T(8,128)}) %all-reduce.4.cloned.1.call-update) | async-done | bytes 2097168 | tf_op jit(solution)/shard_map/psum | solution.py:107
  259.3 4.4 all-to-all-start.3
  263.9 12.9 %all-to-all-done.3 = bf16[16,64,512]{2,1,0:T(8,128)(2,1)} async-done(((bf16[16,64,512]{2,1,0:T(8,128)(2,1)}), bf16[16,64,512]{2,1,0:T(8,128)(2,1)}, u32[]{:S(2)}, u32[]{:S(2)}) %all-to-all-start.3) | async-done | bytes 1048608 | tf_op jit(solution)/shard_map/all_to_all | solution.py:65
  278.4 92.2 %while.41 = (s32[]{:T(128)}, f32[1024,512]{1,0:T(8,128)}, s32[8,3]{0,1:T(4,128)S(1)}, s32[]{:T(128)}, bf16[8,64,4096]{2,1,0:T(8,128)(2,1)}, /*index=5*/s32[]{:T(...) while((s32[]{:T(128)}, f32[1024,512]{1,0:T(8,128)}, ...), condition=%wide.region_7.8_spmd, body=%wide.region_6.7_spmd.sunk | while | flops 546144256 | bytes 9110887 | solution.py:49
  285.6 4.4 fusion.123
  297.1 4.4 fusion.123
  308.6 4.4 fusion.123
  320.1 4.4 fusion.123
  331.6 4.4 fusion.123
  343.2 4.4 fusion.123
  370.6 59.9 %all-reduce.6.cloned.1.call-done = f32[1024,512]{1,0:T(8,128)} async-done(((f32[1024,512]{1,0:T(8,128)}), f32[1024,512]{1,0:T(8,128)}) %all-reduce.6.cloned.1.call-update) | async-done | bytes 2097168 | tf_op jit(solution)/shard_map/psum | solution.py:122
  435.6 74.6 %while.42 = (s32[]{:T(128)}, f32[1024,512]{1,0:T(8,128)}, s32[8,3]{0,1:T(4,128)S(1)}, s32[]{:T(128)}, bf16[8,64,4096]{2,1,0:T(8,128)(2,1)}, /*index=5*/s32[]{:T(...) while((s32[]{:T(128)}, f32[1024,512]{1,0:T(8,128)}, ...), condition=%wide.region_10.11_spmd, body=%wide.region_9.10_spmd.sunk | while | flops 546144256 | bytes 15402399 | solution.py:49
  510.2 101.5 %all-reduce.8.cloned.1.call-done = f32[1024,512]{1,0:T(8,128)} async-done(((f32[1024,512]{1,0:T(8,128)}), f32[1024,512]{1,0:T(8,128)}) %all-reduce.8.cloned.1.call-update) | async-done | bytes 2097168 | tf_op jit(solution)/shard_map/psum | solution.py:133
  (248 shorter events, 184.6 us)
Async XLA Ops:
  10.6 8.0 %all-to-all-start = ((s32[2,8,1]{1,2,0:T(1,128)}), s32[2,8,1]{1,2,0:T(1,128)S(1)}, u32[]{:S(2)}, u32[]{:S(2)}) async-start(s32[2,8,1]{1,2,0:T(1,128)} %bitcast.29), calls=%async_computation | async-start | bytes 2048 | tf_op jit(solution)/shard_map/all_to_all | solution.py:83
  20.3 16.5 %all-to-all-start.1 = ((bf16[16,64,512]{2,1,0:T(8,128)(2,1)}), bf16[16,64,512]{2,1,0:T(8,128)(2,1)S(1)}, u32[]{:S(2)}, u32[]{:S(2)}) async-start(bf16[16,64,512]{2,1,0:T(8,128)(2,1)} %gather_fusion), calls=%async_computation.1 | async-start | bytes 2097152 | tf_op jit(solution)/shard_map/all_to_all | solution.py:65
  44.1 5.1 copy-start.7
  54.8 5.1 copy-start.7
  65.6 5.1 copy-start.7
  76.4 5.1 copy-start.7
  87.2 5.1 copy-start.7
  98.0 5.1 copy-start.7
  108.8 5.1 copy-start.7
  119.6 5.1 copy-start.7
  124.6 27.0 %all-to-all-start.2 = ((f32[16,64,512]{2,1,0:T(8,128)}), f32[16,64,512]{2,1,0:T(8,128)S(1)}, u32[]{:S(2)}, u32[]{:S(2)}) async-start(f32[16,64,512]{2,1,0:T(8,128)} %bitcast.175), calls=%async_computation.2 | async-start | bytes 4194304 | tf_op jit(solution)/shard_map/all_to_all | solution.py:96
  128.4 125.9 %all-reduce.4.cloned.1.call-start = ((), (), s32[]{:S(2)}) async-start(), calls=%async_computation.4 | async-start | bytes 4194304 | tf_op jit(solution)/shard_map/psum | solution.py:107
  155.5 98.8 %copy-start = (f32[1024,512]{1,0:T(8,128)S(1)}, f32[1024,512]{1,0:T(8,128)}, u32[]{:S(2)}) copy-start(f32[1024,512]{1,0:T(8,128)} %param.15) | copy-start | bytes 6291460
  259.3 17.6 %all-to-all-start.3 = ((bf16[16,64,512]{2,1,0:T(8,128)(2,1)}), bf16[16,64,512]{2,1,0:T(8,128)(2,1)}, u32[]{:S(2)}, u32[]{:S(2)}) async-start(bf16[16,64,512]{2,1,0:T(8,128)(2,1)} %gather_fusion.1), calls=%async_computation.3 | async-start | bytes 2097152 | tf_op jit(solution)/shard_map/all_to_all | solution.py:65
  263.7 166.9 %all-reduce.6.cloned.1.call-start = ((), (), s32[]{:S(2)}) async-start(), calls=%async_computation.5 | async-start | bytes 4194304 | tf_op jit(solution)/shard_map/psum | solution.py:122
  370.6 60.0 %copy-start.2 = (f32[1024,512]{1,0:T(8,128)S(1)}, f32[1024,512]{1,0:T(8,128)}, u32[]{:S(2)}) copy-start(f32[1024,512]{1,0:T(8,128)} %param.16) | copy-start | bytes 6291460
  370.6 241.1 %all-reduce.8.cloned.1.call-start = ((), (), s32[]{:S(2)}) async-start(), calls=%async_computation.6 | async-start | bytes 4194304 | tf_op jit(solution)/shard_map/psum | solution.py:133
  441.1 3.8 copy-start.5
  469.0 3.8 copy-start.5
  478.4 3.8 copy-start.5
  487.7 3.8 copy-start.5
  497.0 3.8 copy-start.5
  506.4 3.8 copy-start.5
  510.2 101.5 %copy-start.3 = (f32[1024,512]{1,0:T(8,128)S(1)}, f32[1024,512]{1,0:T(8,128)}, u32[]{:S(2)}) copy-start(f32[1024,512]{1,0:T(8,128)} %param.17) | copy-start | bytes 6291460
  (19 other events, 68.8 us)
Sparse Core Ops, SparseCore 0:
  155.6 98.5 all-reduce.3
  370.7 59.7 all-reduce.5
  510.3 101.3 all-reduce.7
where the time goes:
time: 626 us; the launch traced here: 622 us
  waiting for transfers between devices  307 us (49%)
  matrix products  107 us (17%)
  other arithmetic  65.5 us (10%)
  local copies, waits for them, and re-layouts  64.8 us (10%)
  loops' own time  47.1 us (8%)
  starting transfers between devices  16.3 us (3%)
  between operations  13.8 us (2%)
    dot_general x24, matrix products, block_gradient(): jnp.einsum(grad_form, misfit, khatri, preferred_element_type=jnp.float32)  106 us
    psum x1, waiting for transfers between devices, per_device(): third_part = lax.psum(third_part, ('ia', 'ja'))  102 us
    psum x1, waiting for transfers between devices, per_device(): first_part = lax.psum(first_part, ('ja', 'ka'))  98.7 us
    psum x1, waiting for transfers between devices, per_device(): second_part = lax.psum(second_part, ('ia', 'ka'))  59.9 us
    another operation x3, loops' own time, accumulate(): return lax.fori_loop(0, blocks.shape[0], visit, empty)  47.1 us
    convert_element_type x32, local copies, waits for them, and re-layouts, block_gradient(): misfit = (cube.astype(jnp.float32) - model).astype(jnp.bfloat16)  34.5 us
    convert_element_type x24, other arithmetic, block_gradient(): misfit = (cube.astype(jnp.float32) - model).astype(jnp.bfloat16)  26.8 us
    all_to_all x1, waiting for transfers between devices, per_device(): lax.all_to_all(slot_terms.reshape(all_slots, edge, width), 'ia', split_ax...  23.1 us
  transfers between devices with their start and end apart: 7, of which 7 were waited for; matrix products, arithmetic and copies ran while one was open for 1% of the time, Pallas kernels for 0%

commit v1 on v0

--- a/solution.py
+++ b/solution.py
@@ -104,7 +104,8 @@
         precision=lax.Precision.HIGHEST,
         preferred_element_type=jnp.float32,
     ).reshape(span_one, width)
-    first_part = lax.psum(first_part, ("ja", "ka"))
+    half = lax.psum(first_part, "ka")
+    first_part = lax.psum(half, "ja")
     factor_one = factor_one + STEP_SIZE * first_part
     first_rows = serve_rows(incoming, factor_one, edge, held_rows).reshape(
         groups * per_pair * edge, width

time: 626 us -> 669 us (1.069)
  waiting for transfers between devices: 307 us -> 350 us
    psum x1 -> x2, waiting for transfers between devices: 98.7 us -> 140 us  [the longest x1 88.6 us: per_device(): first_part = lax.psum(half, 'ja')]
  transfers between devices with their start and end apart: 7 -> 8, of which waited for: 7 -> 8; matrix products, arithmetic and copies ran while one was open for 1% -> 1% of each run, Pallas kernels for 0% -> 0%
where the time goes in v1:
time: 669 us; the launch traced here: 665 us
  waiting for transfers between devices  350 us (52%)
  matrix products  107 us (16%)
  other arithmetic  65.5 us (10%)
  local copies, waits for them, and re-layouts  64.8 us (10%)
  loops' own time  47.9 us (7%)
  starting transfers between devices  16.4 us (2%)
  between operations  13.8 us (2%)
    dot_general x24, matrix products, block_gradient(): jnp.einsum(grad_form, misfit, khatri, preferred_element_type=jnp.float32)  106 us
    psum x1, waiting for transfers between devices, per_device(): third_part = lax.psum(third_part, ('ia', 'ja'))  102 us
    psum x1, waiting for transfers between devices, per_device(): first_part = lax.psum(half, 'ja')  88.6 us
    psum x1, waiting for transfers between devices, per_device(): second_part = lax.psum(second_part, ('ia', 'ka'))  60.4 us
    psum x1, waiting for transfers between devices, per_device(): half = lax.psum(first_part, 'ka')  51.8 us
    another operation x3, loops' own time, accumulate(): return lax.fori_loop(0, blocks.shape[0], visit, empty)  47.9 us
    convert_element_type x32, local copies, waits for them, and re-layouts, block_gradient(): misfit = (cube.astype(jnp.float32) - model).astype(jnp.bfloat16)  34.5 us
    convert_element_type x24, other arithmetic, block_gradient(): misfit = (cube.astype(jnp.float32) - model).astype(jnp.bfloat16)  26.8 us
  transfers between devices with their start and end apart: 8, of which 8 were waited for; matrix products, arithmetic and copies ran while one was open for 1% of the time, Pallas kernels for 0%

profile of v1, /device:TPU:0, one launch (start us, length us, event | category | flops | bytes accessed | tf_op | source)
XLA Modules:
  0.0 665.1 jit_solution(5888735727909697752)
XLA Ops:
  27.9 8.8 %all-to-all-done.1 = bf16[16,64,512]{2,1,0:T(8,128)(2,1)S(1)} async-done(((bf16[16,64,512]{2,1,0:T(8,128)(2,1)}), bf16[16,64,512]{2,1,0:T(8,128)(2,1)S(1)}, u32[]{:S(2)}, u32[]{:S(2)}) %all-to-all-start.1) | async-done | bytes 1048608 | tf_op jit(solution)/shard_map/all_to_all | solution.py:65
  38.3 84.7 %while.40 = (s32[]{:T(128)}, f32[1024,512]{1,0:T(8,128)}, s32[8,3]{0,1:T(4,128)S(1)}, bf16[8,64,4096]{2,1,0:T(8,128)(2,1)}, bf16[1024,512]{1,0:T(8,128)(2,1)S(1)...) while((s32[]{:T(128)}, f32[1024,512]{1,0:T(8,128)}, ...), condition=%wide.region_4.5_spmd, body=%wide.region_3.4_spmd.sunk | while | flops 546144256 | bytes 15402399 | solution.py:49
  43.9 5.0 fusion.118
  54.5 5.0 fusion.118
  65.1 5.0 fusion.118
  75.6 5.0 fusion.118
  86.2 5.0 fusion.118
  96.8 5.0 fusion.118
  107.4 5.0 fusion.118
  118.0 5.0 fusion.118
  126.9 23.1 %all-to-all-done.2 = f32[16,64,512]{2,1,0:T(8,128)S(1)} async-done(((f32[16,64,512]{2,1,0:T(8,128)}), f32[16,64,512]{2,1,0:T(8,128)S(1)}, u32[]{:S(2)}, u32[]{:S(2)}) %all-to-all-start.2) | async-done | bytes 2097184 | tf_op jit(solution)/shard_map/all_to_all | solution.py:96
  154.0 51.8 %all-reduce.5.cloned.1.call-done = f32[1024,512]{1,0:T(8,128)} async-done(((f32[1024,512]{1,0:T(8,128)}), f32[1024,512]{1,0:T(8,128)}) %all-reduce.5.cloned.1.call-update) | async-done | bytes 2097168 | tf_op jit(solution)/shard_map/psum | solution.py:107
  205.8 88.6 %all-reduce.7.cloned.1.call-done = f32[1024,512]{1,0:T(8,128)} async-done(((f32[1024,512]{1,0:T(8,128)}), f32[1024,512]{1,0:T(8,128)}) %all-reduce.7.cloned.1.call-update) | async-done | bytes 2097168 | tf_op jit(solution)/shard_map/psum | solution.py:108
  299.4 4.4 all-to-all-start.3
  304.1 13.4 %all-to-all-done.3 = bf16[16,64,512]{2,1,0:T(8,128)(2,1)} async-done(((bf16[16,64,512]{2,1,0:T(8,128)(2,1)}), bf16[16,64,512]{2,1,0:T(8,128)(2,1)}, u32[]{:S(2)}, u32[]{:S(2)}) %all-to-all-start.3) | async-done | bytes 1048608 | tf_op jit(solution)/shard_map/all_to_all | solution.py:65
  319.1 94.3 %while.41 = (s32[]{:T(128)}, f32[1024,512]{1,0:T(8,128)}, s32[8,3]{0,1:T(4,128)S(1)}, s32[]{:T(128)}, bf16[8,64,4096]{2,1,0:T(8,128)(2,1)}, /*index=5*/s32[]{:T(...) while((s32[]{:T(128)}, f32[1024,512]{1,0:T(8,128)}, ...), condition=%wide.region_8.9_spmd, body=%wide.region_7.8_spmd.sunk | while | flops 546144256 | bytes 9110887 | solution.py:49
  326.5 4.4 fusion.123
  350.0 4.4 fusion.123
  361.8 4.4 fusion.123
  373.6 4.4 fusion.123
  397.2 4.4 fusion.123
  413.4 60.4 %all-reduce.9.cloned.1.call-done = f32[1024,512]{1,0:T(8,128)} async-done(((f32[1024,512]{1,0:T(8,128)}), f32[1024,512]{1,0:T(8,128)}) %all-reduce.9.cloned.1.call-update) | async-done | bytes 2097168 | tf_op jit(solution)/shard_map/psum | solution.py:123
  478.8 74.8 %while.42 = (s32[]{:T(128)}, f32[1024,512]{1,0:T(8,128)}, s32[8,3]{0,1:T(4,128)S(1)}, s32[]{:T(128)}, bf16[8,64,4096]{2,1,0:T(8,128)(2,1)}, /*index=5*/s32[]{:T(...) while((s32[]{:T(128)}, f32[1024,512]{1,0:T(8,128)}, ...), condition=%wide.region_11.12_spmd, body=%wide.region_10.11_spmd.sunk | while | flops 546144256 | bytes 15402399 | solution.py:49
  553.7 101.5 %all-reduce.11.cloned.1.call-done = f32[1024,512]{1,0:T(8,128)} async-done(((f32[1024,512]{1,0:T(8,128)}), f32[1024,512]{1,0:T(8,128)}) %all-reduce.11.cloned.1.call-update) | async-done | bytes 2097168 | tf_op jit(solution)/shard_map/psum | solution.py:134
  (251 shorter events, 189.1 us)
Async XLA Ops:
  10.6 8.0 %all-to-all-start = ((s32[2,8,1]{1,2,0:T(1,128)}), s32[2,8,1]{1,2,0:T(1,128)S(1)}, u32[]{:S(2)}, u32[]{:S(2)}) async-start(s32[2,8,1]{1,2,0:T(1,128)} %bitcast.29), calls=%async_computation | async-start | bytes 2048 | tf_op jit(solution)/shard_map/all_to_all | solution.py:83
  20.3 16.5 %all-to-all-start.1 = ((bf16[16,64,512]{2,1,0:T(8,128)(2,1)}), bf16[16,64,512]{2,1,0:T(8,128)(2,1)S(1)}, u32[]{:S(2)}, u32[]{:S(2)}) async-start(bf16[16,64,512]{2,1,0:T(8,128)(2,1)} %gather_fusion), calls=%async_computation.1 | async-start | bytes 2097152 | tf_op jit(solution)/shard_map/all_to_all | solution.py:65
  43.9 5.1 copy-start.7
  54.4 5.1 copy-start.7
  65.0 5.1 copy-start.7
  75.6 5.1 copy-start.7
  86.2 5.1 copy-start.7
  96.8 5.1 copy-start.7
  107.4 5.1 copy-start.7
  118.0 5.1 copy-start.7
  123.0 27.0 %all-to-all-start.2 = ((f32[16,64,512]{2,1,0:T(8,128)}), f32[16,64,512]{2,1,0:T(8,128)S(1)}, u32[]{:S(2)}, u32[]{:S(2)}) async-start(f32[16,64,512]{2,1,0:T(8,128)} %bitcast.175), calls=%async_computation.2 | async-start | bytes 4194304 | tf_op jit(solution)/shard_map/all_to_all | solution.py:96
  126.8 79.0 %all-reduce.5.cloned.1.call-start = ((), (), s32[]{:S(2)}) async-start(), calls=%async_computation.4 | async-start | bytes 4194304 | tf_op jit(solution)/shard_map/psum | solution.py:107
  153.9 140.5 %copy-start = (f32[1024,512]{1,0:T(8,128)S(1)}, f32[1024,512]{1,0:T(8,128)}, u32[]{:S(2)}) copy-start(f32[1024,512]{1,0:T(8,128)} %param.15) | copy-start | bytes 6291460
  154.0 140.5 %all-reduce.7.cloned.1.call-start = ((), (), s32[]{:S(2)}) async-start(), calls=%async_computation.5 | async-start | bytes 4194304 | tf_op jit(solution)/shard_map/psum | solution.py:108
  299.4 18.1 %all-to-all-start.3 = ((bf16[16,64,512]{2,1,0:T(8,128)(2,1)}), bf16[16,64,512]{2,1,0:T(8,128)(2,1)}, u32[]{:S(2)}, u32[]{:S(2)}) async-start(bf16[16,64,512]{2,1,0:T(8,128)(2,1)} %gather_fusion.1), calls=%async_computation.3 | async-start | bytes 2097152 | tf_op jit(solution)/shard_map/all_to_all | solution.py:65
  303.9 170.0 %all-reduce.9.cloned.1.call-start = ((), (), s32[]{:S(2)}) async-start(), calls=%async_computation.6 | async-start | bytes 4194304 | tf_op jit(solution)/shard_map/psum | solution.py:123
  413.4 60.5 %copy-start.2 = (f32[1024,512]{1,0:T(8,128)S(1)}, f32[1024,512]{1,0:T(8,128)}, u32[]{:S(2)}) copy-start(f32[1024,512]{1,0:T(8,128)} %param.16) | copy-start | bytes 6291460
  413.4 241.8 %all-reduce.11.cloned.1.call-start = ((), (), s32[]{:S(2)}) async-start(), calls=%async_computation.7 | async-start | bytes 4194304 | tf_op jit(solution)/shard_map/psum | solution.py:134
  493.7 3.8 copy-start.5
  503.1 3.8 copy-start.5
  512.4 3.8 copy-start.5
  521.8 3.8 copy-start.5
  549.8 3.8 copy-start.5
  553.7 101.5 %copy-start.3 = (f32[1024,512]{1,0:T(8,128)S(1)}, f32[1024,512]{1,0:T(8,128)}, u32[]{:S(2)}) copy-start(f32[1024,512]{1,0:T(8,128)} %param.17) | copy-start | bytes 6291460
  (20 other events, 71.4 us)
Sparse Core Ops, SparseCore 0:
  154.1 51.6 all-reduce.4
  208.2 86.1 all-reduce.6
  413.5 60.2 all-reduce.8
  553.8 101.3 all-reduce.10
